TPU v7x, 512 devices: a whole 4x8x8 slice. The times are simulated.
512 devices in a mesh: row: 32 (over x, y), col: 16 (over z, core).
Axes of the slice: x: 4, y: 8, z: 8, core: 2. Of those that a mesh axis runs over, the one named last changes fastest.
Arguments:
- features: bfloat16 [131072, 128], P(('row', 'col')), may hold values from -6 to 6
- degree: int32 [131072], P(('row', 'col')), may hold values from 1 to 256
- weight: bfloat16 [128, 128], replicated, may hold values from -0.5 to 0.5
- bias: float32 [128], replicated, may hold values from -3 to 3
- cotangent: bfloat16 [131072, 128], P(('row', 'col')), may hold values from -8 to 8
- tile_rows: int32 [32, 16, 128], P('row', 'col'), may hold values from 0 to 31
- tile_cols: int32 [32, 16, 128], P('row', 'col'), may hold values from 0 to 63
- tile_count: int32 [32, 16, 1], P('row', 'col'), may hold values from 32 to 128, as said below
- tile_codes: int32 [32, 16, 128, 256], P('row', 'col'), may hold values from 0 to 4095
Outputs:
- hidden: bfloat16 [131072, 128], P(('row', 'col'))
- grad_features: bfloat16 [131072, 128], P(('row', 'col'))
- grad_weight: float32 [128, 128], replicated
- grad_bias: float32 [128], replicated
Inputs may be any that keep to these rules, and one draw needn't show every extreme that they name: Only the first tile_count slots of a block are live; on some block the count is exactly 128. `tile_rows`: A tile position may repeat within a block; repeated tiles add.
All inputs are finite; a program needn't handle non-finite values.
Results may differ from a plain program's by a relative error of at most 0.019.
Values may be sent and summed in bfloat16 or wider, within the bound.
A program may use at most 64 MiB of HBM per device.

v0:
```python
import math
import jax
import jax.numpy as jnp
from jax import lax
from jax.sharding import PartitionSpec as P

BLOCK = 16


def tile_mask(code_block, living):
    tile_side = code_block.shape[1] // 2
    row_code = code_block[:, :tile_side][:, :, None]
    col_code = code_block[:, tile_side:][:, None, :]
    hashed = (row_code * col_code + row_code + 3 * col_code) % 4093
    return ((hashed < 64) & living[:, None, None]).astype(jnp.bfloat16)


def accumulate(codes_dev, rows_dev, cols_dev, count_dev, source, out_tiles, backward):
    tile_side = source.shape[1]
    width_feat = source.shape[2]

    def block_step(block_id, summed):
        slot_start = block_id * BLOCK
        code_block = lax.dynamic_slice_in_dim(codes_dev, slot_start, BLOCK, 0)
        row_block = lax.dynamic_slice_in_dim(rows_dev, slot_start, BLOCK, 0)
        col_block = lax.dynamic_slice_in_dim(cols_dev, slot_start, BLOCK, 0)
        slot_ids = slot_start + jnp.arange(BLOCK, dtype=jnp.int32)
        target = col_block if backward else row_block
        anchor = row_block if backward else col_block
        living = slot_ids < count_dev
        keep = tile_mask(code_block, living)
        picked = jnp.take(source, anchor, axis=0)
        if backward:
            product = jnp.einsum("tij,tif->tjf", keep, picked, preferred_element_type=jnp.float32)
        else:
            product = jnp.einsum("tij,tjf->tif", keep, picked, preferred_element_type=jnp.float32)
        return summed.at[target].add(product)

    start_sum = jnp.zeros((out_tiles, tile_side, width_feat), jnp.float32)
    loop_count = codes_dev.shape[0] // BLOCK
    summed = lax.fori_loop(0, loop_count, block_step, start_sum)
    return summed.reshape(out_tiles * tile_side, width_feat)


def dense_part(aggregate, weight, bias, cotangent, inv_root):
    preact = jnp.dot(aggregate, weight, preferred_element_type=jnp.float32) + bias
    hidden = jax.nn.elu(preact).astype(jnp.bfloat16)
    elu_slope = jnp.where(preact > 0, 1.0, jnp.exp(jnp.minimum(preact, 0.0)))
    grad_pre = cotangent.astype(jnp.float32) * elu_slope
    grad_pre_b = grad_pre.astype(jnp.bfloat16)
    grad_weight = lax.dot_general(
        aggregate, grad_pre_b, (((0,), (0,)), ((), ())), preferred_element_type=jnp.float32
    )
    grad_bias = jnp.sum(grad_pre, axis=0)
    grad_agg = jnp.dot(grad_pre_b, weight.T, preferred_element_type=jnp.float32)
    grad_scaled = (inv_root * grad_agg).astype(jnp.bfloat16)
    return (hidden, grad_weight, grad_bias, grad_scaled)


def local(features, degree, weight, bias, cotangent, tile_rows, tile_cols, tile_count, tile_codes):
    codes_dev = tile_codes[0, 0]
    rows_dev = tile_rows[0, 0]
    cols_dev = tile_cols[0, 0]
    count_dev = tile_count[0, 0, 0]
    pieces = features.shape[0]
    width_feat = features.shape[1]
    tile_side = codes_dev.shape[1] // 2
    row_devs = lax.axis_size("row")
    col_devs = lax.axis_size("col")
    grad_scale = 1.0 / math.sqrt(pieces * row_devs * col_devs)
    row_tiles = pieces * col_devs // tile_side
    col_tiles = pieces * row_devs // tile_side
    inv_root = lax.rsqrt(degree.astype(jnp.float32))[:, None]
    scaled = (inv_root * features.astype(jnp.float32)).astype(jnp.bfloat16)
    column_feats = lax.all_gather(scaled, "row", axis=0, tiled=True).reshape(
        col_tiles, tile_side, width_feat
    )
    row_terms = accumulate(codes_dev, rows_dev, cols_dev, count_dev, column_feats, row_tiles, False)
    agg_sum = lax.psum_scatter(
        row_terms.astype(jnp.bfloat16), "col", scatter_dimension=0, tiled=True
    ).astype(jnp.float32)
    aggregate = (inv_root * agg_sum).astype(jnp.bfloat16)
    hidden, grad_weight, grad_bias, grad_scaled = dense_part(
        aggregate, weight, bias, cotangent, inv_root
    )
    grad_weight, grad_bias = lax.psum(
        (grad_weight * grad_scale, grad_bias * grad_scale), ("row", "col")
    )
    row_grads = lax.all_gather(grad_scaled, "col", axis=0, tiled=True)
    row_sources = row_grads.reshape(row_tiles, tile_side, width_feat)
    col_terms = accumulate(codes_dev, rows_dev, cols_dev, count_dev, row_sources, col_tiles, True)
    grad_sum = lax.psum_scatter(
        col_terms.astype(jnp.bfloat16), "row", scatter_dimension=0, tiled=True
    ).astype(jnp.float32)
    grad_features = (inv_root * grad_sum).astype(jnp.bfloat16)
    return (hidden, grad_features, grad_weight, grad_bias)


def solution(mesh):
    placed = (
        P(("row", "col"), None),
        P(("row", "col")),
        P(),
        P(),
        P(("row", "col"), None),
        P("row", "col", None),
        P("row", "col", None),
        P("row", "col", None),
        P("row", "col", None, None),
    )
    return jax.shard_map(
        local,
        mesh=mesh,
        in_specs=placed,
        out_specs=(P(("row", "col"), None), P(("row", "col"), None), P(), P()),
        check_vma=False,
    )
```

profile of v0, /device:TPU:1, one launch (start us, length us, event | category | flops | bytes accessed | tf_op | source)
XLA Modules:
  0.0 838.8 jit_solution(7499523494927583328)
XLA Ops:
  9.6 86.1 %all-gather.3.cloned.1.call-done = bf16[8192,128]{1,0:T(8,128)(2,1)} async-done(((bf16[256,128]{1,0:T(8,128)(2,1)}), bf16[8192,128]{1,0:T(8,128)(2,1)}) %all-gather.3.cloned.1.call-update) | async-done | bytes 2097168 | tf_op jit(solution)/shard_map/all_gather | solution.py:75
  96.0 66.9 %while.30 = (s32[]{:T(128)}, f32[32,128,128]{2,1,0:T(8,128)S(1)}, s32[128]{0:T(128)S(1)}, s32[128,256]{1,0:T(8,128)}, s32[]{:T(128)}, /*index=5*/s32[128]{0:T(12...) while((s32[]{:T(128)}, f32[32,128,128]{2,1,0:T(8,128)S(1)}, ...), condition=%wide.region_2.3_spmd, body=%wide.region_0.2_spmd.sunk | while | flops 70519992 | bytes 5837511 | solution.py:41
  97.5 3.0 gather_fusion
  105.9 3.0 gather_fusion
  114.2 3.0 gather_fusion
  122.6 3.0 gather_fusion
  131.0 3.0 gather_fusion
  139.3 3.0 gather_fusion
  156.1 3.0 gather_fusion
  164.1 61.1 %reduce-scatter.3.cloned.1.call-done = bf16[256,128]{1,0:T(8,128)(2,1)} async-done(((bf16[4096,128]{1,0:T(8,128)(2,1)}), bf16[256,128]{1,0:T(8,128)(2,1)}) %reduce-scatter.3.cloned.1.call-update) | async-done | bytes 65552 | tf_op jit(solution)/shard_map/reduce_scatter | solution.py:79
  227.9 43.0 %all-gather.5.cloned.1.call-done = bf16[4096,128]{1,0:T(8,128)(2,1)} async-done(((bf16[256,128]{1,0:T(8,128)(2,1)}), bf16[4096,128]{1,0:T(8,128)(2,1)}) %all-gather.5.cloned.1.call-update) | async-done | bytes 1048592 | tf_op jit(solution)/shard_map/all_gather | solution.py:89
  273.4 63.9 %while.31 = (s32[]{:T(128)}, f32[64,128,128]{2,1,0:T(8,128)}, s32[128]{0:T(128)S(1)}, s32[128,256]{1,0:T(8,128)}, s32[]{:T(128)}, /*index=5*/s32[128]{0:T(128)S(...) while((s32[]{:T(128)}, f32[64,128,128]{2,1,0:T(8,128)}, ...), condition=%wide.region_6.7_spmd, body=%wide.region_4.6_spmd.sunk | while | flops 70519992 | bytes 5837511 | solution.py:41
  278.0 3.4 scatter_fusion.1
  286.0 3.4 scatter_fusion.1
  293.9 3.4 scatter_fusion.1
  301.9 3.4 scatter_fusion.1
  309.9 3.4 scatter_fusion.1
  317.9 3.4 scatter_fusion.1
  325.9 3.4 scatter_fusion.1
  333.9 3.4 scatter_fusion.1
  337.3 3.9 convert_element_type.62
  341.3 98.5 %psum.15 = f32[128]{0:T(128)} all-reduce(f32[128]{0:T(128)S(1)} %broadcast_multiply_fusion.2), channel_id=1, replica_groups=mesh['row'=32,'col'=16] {'row','col'}, use_global_device_ids=true, to_apply=%region_10.11 | all-reduce | flops 128 | bytes 1024 | tf_op jit(solution)/shard_map/psum | solution.py:86
  440.7 117.3 %reduce-scatter.5.cloned.1.call-done = bf16[256,128]{1,0:T(8,128)(2,1)} async-done(((bf16[8192,128]{1,0:T(8,128)(2,1)}), bf16[256,128]{1,0:T(8,128)(2,1)}) %reduce-scatter.5.cloned.1.call-update) | async-done | bytes 65552 | tf_op jit(solution)/shard_map/reduce_scatter | solution.py:92
  559.6 271.2 %all-reduce.2.cloned.1.call-done = f32[128,128]{1,0:T(8,128)} async-done(((f32[128,128]{1,0:T(8,128)}), f32[128,128]{1,0:T(8,128)}) %all-reduce.2.cloned.1.call-update) | async-done | bytes 65552 | tf_op jit(solution)/shard_map/psum | solution.py:86
  (132 shorter events, 95.1 us)
Async XLA Ops:
  7.2 218.1 %copy-start = (bf16[128,128]{1,0:T(8,128)(2,1)S(1)}, bf16[128,128]{1,0:T(8,128)(2,1)}, u32[]{:S(2)}) copy-start(bf16[128,128]{1,0:T(8,128)(2,1)} %param.15) | copy-start | bytes 98308
  7.2 88.8 %copy-start.3 = (s32[1,1,128]{2,1,0:T(1,128)S(1)}, s32[1,1,128]{2,1,0:T(1,128)}, u32[]{:S(2)}) copy-start(s32[1,1,128]{2,1,0:T(1,128)} %param.19) | copy-start | bytes 1540
  7.2 88.8 %copy-start.2 = (s32[1,1,128]{2,1,0:T(1,128)S(1)}, s32[1,1,128]{2,1,0:T(1,128)}, u32[]{:S(2)}) copy-start(s32[1,1,128]{2,1,0:T(1,128)} %param.18) | copy-start | bytes 1540
  7.2 88.5 %all-gather.3.cloned.1.call-start = ((), (), s32[]{:S(2)}) async-start(), calls=%async_computation.2 | async-start | bytes 2162688 | tf_op jit(solution)/shard_map/all_gather | solution.py:75
  9.5 215.7 %reduce-scatter.3.cloned.1.call-start = ((), (), s32[]{:S(2)}) async-start(), calls=%async_computation.3 | async-start | bytes 1114112 | tf_op jit(solution)/shard_map/reduce_scatter | solution.py:79
  162.9 62.3 %copy-start.4 = (bf16[256,128]{1,0:T(8,128)(2,1)S(1)}, bf16[256,128]{1,0:T(8,128)(2,1)}, u32[]{:S(2)}) copy-start(bf16[256,128]{1,0:T(8,128)(2,1)} %param.17) | copy-start | bytes 196612
  162.9 62.3 %copy-start.6 = (f32[128]{0:T(128)S(1)}, f32[128]{0:T(128)}, u32[]{:S(2)}) copy-start(f32[128]{0:T(128)} %param.16) | copy-start | bytes 1540
  164.1 106.8 %all-gather.5.cloned.1.call-start = ((), (), s32[]{:S(2)}) async-start(), calls=%async_computation.4 | async-start | bytes 1114112 | tf_op jit(solution)/shard_map/all_gather | solution.py:89
  227.8 330.2 %reduce-scatter.5.cloned.1.call-start = ((), (), s32[]{:S(2)}) async-start(), calls=%async_computation.5 | async-start | bytes 2162688 | tf_op jit(solution)/shard_map/reduce_scatter | solution.py:92
  270.9 2.5 copy-start.1
  341.2 98.6 %copy-start.5 = (bf16[256,128]{1,0:T(8,128)(2,1)S(1)}, bf16[256,128]{1,0:T(8,128)(2,1)}, u32[]{:S(2)}) copy-start(bf16[256,128]{1,0:T(8,128)(2,1)} %reduce-scatter.3.cloned.1.call-done) | copy-start | bytes 196612
  341.2 489.6 %all-reduce.2.cloned.1.call-start = ((), (), s32[]{:S(2)}) async-start(), calls=%async_computation.6 | async-start | bytes 131072 | tf_op jit(solution)/shard_map/psum | solution.py:86
Sparse Core Ops, SparseCore 0:
  11.8 83.9 all-gather.2
  164.2 60.9 reduce-scatter.2
  227.9 42.9 all-gather.4
  341.3 216.6 reduce-scatter.4
  563.4 267.3 all-reduce.1
where the time goes:
time: 841 us; the launch traced here: 839 us
  waiting for transfers between devices  579 us (69%)
  blocking collectives  98.5 us (12%)
  other arithmetic  73.3 us (9%)
  matrix products  40.1 us (5%)
  local copies, waits for them, and re-layouts  33.5 us (4%)
  between operations  13.9 us (2%)
    psum x1, waiting for transfers between devices, local(): lax.psum((grad_weight * grad_scale, grad_bias * grad_scale), ('row', 'col'))  271 us
    reduce_scatter x1, waiting for transfers between devices, local(): lax.psum_scatter(col_terms.astype(jnp.bfloat16), 'row', scatter_dimension...  117 us
    psum x1, blocking collectives, local(): lax.psum((grad_weight * grad_scale, grad_bias * grad_scale), ('row', 'col'))  98.5 us
    all_gather x1, waiting for transfers between devices, local(): lax.all_gather(scaled, 'row', axis=0, tiled=True)  86.1 us
    reduce_scatter x1, waiting for transfers between devices, local(): lax.psum_scatter(row_terms.astype(jnp.bfloat16), 'col', scatter_dimension...  61.1 us
    all_gather x1, waiting for transfers between devices, local(): row_grads = lax.all_gather(grad_scaled, 'col', axis=0, tiled=True)  43 us
    scatter-add x16, other arithmetic, block_step(): return summed.at[target].add(product)  39.9 us
    gather x16, local copies, waits for them, and re-layouts, block_step(): picked = jnp.take(source, anchor, axis=0)  29.3 us
  transfers between devices with their start and end apart: 5, of which 5 were waited for; matrix products, arithmetic and copies ran while one was open for 0% of the time, Pallas kernels for 0%

commit v1 on v0

--- a/solution.py
+++ b/solution.py
@@ -84,7 +84,7 @@
         aggregate, weight, bias, cotangent, inv_root
     )
     grad_weight, grad_bias = lax.psum(
-        (grad_weight * grad_scale, grad_bias * grad_scale), ("row", "col")
+        lax.psum((grad_weight * grad_scale, grad_bias * grad_scale), "row"), "col"
     )
     row_grads = lax.all_gather(grad_scaled, "col", axis=0, tiled=True)
     row_sources = row_grads.reshape(row_tiles, tile_side, width_feat)

time: 841 us -> 770 us (0.916)
  waiting for transfers between devices: 579 us -> 507 us
    psum x1 -> x2, waiting for transfers between devices: 271 us -> 111 us  [the longest x1 111 us: local(): lax.psum(lax.psum((grad_weight * grad_scale, grad_bias * grad_scale), 'ro...]
    reduce_scatter x1, waiting for transfers between devices: 117 us -> 207 us  [local(): lax.psum_scatter(col_terms.astype(jnp.bfloat16), 'row', scatter_dimension...]
    psum x1 -> x2, blocking collectives: 98.5 us -> 98.5 us  [the longest x1 60.6 us: local(): lax.psum((grad_weight * grad_scale, grad_bias * grad_scale), 'row')]
  transfers between devices with their start and end apart: 5 -> 6, of which waited for: 5 -> 5; matrix products, arithmetic and copies ran while one was open for 0% -> 10% of each run, Pallas kernels for 0% -> 0%
where the time goes in v1:
time: 770 us; the launch traced here: 768 us
  waiting for transfers between devices  507 us (66%)
  blocking collectives  98.5 us (13%)
  other arithmetic  73.3 us (10%)
  matrix products  41 us (5%)
  local copies, waits for them, and re-layouts  33.3 us (4%)
  between operations  14.2 us (2%)
    reduce_scatter x1, waiting for transfers between devices, local(): lax.psum_scatter(col_terms.astype(jnp.bfloat16), 'row', scatter_dimension...  207 us
    psum x1, waiting for transfers between devices, local(): lax.psum(lax.psum((grad_weight * grad_scale, grad_bias * grad_scale), 'ro...  111 us
    all_gather x1, waiting for transfers between devices, local(): lax.all_gather(scaled, 'row', axis=0, tiled=True)  86.1 us
    reduce_scatter x1, waiting for transfers between devices, local(): lax.psum_scatter(row_terms.astype(jnp.bfloat16), 'col', scatter_dimension...  61.1 us
    psum x1, blocking collectives, local(): lax.psum((grad_weight * grad_scale, grad_bias * grad_scale), 'row')  60.6 us
    all_gather x1, waiting for transfers between devices, local(): row_grads = lax.all_gather(grad_scaled, 'col', axis=0, tiled=True)  41.2 us
    scatter-add x16, other arithmetic, block_step(): return summed.at[target].add(product)  40 us
    psum x1, blocking collectives, local(): lax.psum(lax.psum((grad_weight * grad_scale, grad_bias * grad_scale), 'ro...  37.9 us
  transfers between devices with their start and end apart: 6, of which 5 were waited for; matrix products, arithmetic and copies ran while one was open for 10% of the time, Pallas kernels for 0%

profile of v1, /device:TPU:1, one launch (start us, length us, event | category | flops | bytes accessed | tf_op | source)
XLA Modules:
  0.0 767.9 jit_solution(11202289678529137173)
XLA Ops:
  9.6 86.1 %all-gather.3.cloned.1.call-done = bf16[8192,128]{1,0:T(8,128)(2,1)} async-done(((bf16[256,128]{1,0:T(8,128)(2,1)}), bf16[8192,128]{1,0:T(8,128)(2,1)}) %all-gather.3.cloned.1.call-update) | async-done | bytes 2097168 | tf_op jit(solution)/shard_map/all_gather | solution.py:75
  96.0 66.8 %while.30 = (s32[]{:T(128)}, f32[32,128,128]{2,1,0:T(8,128)S(1)}, s32[128]{0:T(128)S(1)}, s32[128,256]{1,0:T(8,128)}, s32[]{:T(128)}, /*index=5*/s32[128]{0:T(12...) while((s32[]{:T(128)}, f32[32,128,128]{2,1,0:T(8,128)S(1)}, ...), condition=%wide.region_2.3_spmd, body=%wide.region_0.2_spmd.sunk | while | flops 70519992 | bytes 5837511 | solution.py:41
  97.5 3.0 gather_fusion
  105.9 3.0 gather_fusion
  114.2 3.0 gather_fusion
  122.6 3.0 gather_fusion
  130.9 3.0 gather_fusion
  155.9 3.0 gather_fusion
  164.0 61.1 %reduce-scatter.3.cloned.1.call-done = bf16[256,128]{1,0:T(8,128)(2,1)} async-done(((bf16[4096,128]{1,0:T(8,128)(2,1)}), bf16[256,128]{1,0:T(8,128)(2,1)}) %reduce-scatter.3.cloned.1.call-update) | async-done | bytes 65552 | tf_op jit(solution)/shard_map/reduce_scatter | solution.py:79
  229.5 41.2 %all-gather.5.cloned.1.call-done = bf16[4096,128]{1,0:T(8,128)(2,1)} async-done(((bf16[256,128]{1,0:T(8,128)(2,1)}), bf16[4096,128]{1,0:T(8,128)(2,1)}) %all-gather.5.cloned.1.call-update) | async-done | bytes 1048592 | tf_op jit(solution)/shard_map/all_gather | solution.py:89
  273.2 64.0 %while.31 = (s32[]{:T(128)}, f32[64,128,128]{2,1,0:T(8,128)}, s32[128]{0:T(128)S(1)}, s32[128,256]{1,0:T(8,128)}, s32[]{:T(128)}, /*index=5*/s32[128]{0:T(128)S(...) while((s32[]{:T(128)}, f32[64,128,128]{2,1,0:T(8,128)}, ...), condition=%wide.region_6.7_spmd, body=%wide.region_4.6_spmd.sunk | while | flops 70519992 | bytes 5837511 | solution.py:41
  277.8 3.4 scatter_fusion.1
  285.8 3.4 scatter_fusion.1
  293.8 3.4 scatter_fusion.1
  301.7 3.4 scatter_fusion.1
  309.7 3.4 scatter_fusion.1
  317.7 3.4 scatter_fusion.1
  325.8 3.4 scatter_fusion.1
  333.7 3.4 scatter_fusion.1
  337.2 3.9 convert_element_type.62
  341.1 60.6 %psum.30 = f32[128]{0:T(128)S(1)} all-reduce(f32[128]{0:T(128)S(1)} %broadcast_multiply_fusion.2), channel_id=1, replica_groups=mesh['row'=32,'col'=16] {'row'}, use_global_device_ids=true, to_apply=%region_11.12 | all-reduce | flops 128 | bytes 1024 | tf_op jit(solution)/shard_map/psum | solution.py:87
  401.8 37.9 %psum.31 = f32[128]{0:T(128)} all-reduce(f32[128]{0:T(128)S(1)} %psum.30), channel_id=1, replica_groups=mesh['row'=32,'col'=16] {'col'}, use_global_device_ids=true, to_apply=%region_12.13 | all-reduce | flops 128 | bytes 1024 | tf_op jit(solution)/shard_map/psum | solution.py:86
  439.7 207.1 %reduce-scatter.5.cloned.1.call-done = bf16[256,128]{1,0:T(8,128)(2,1)} async-done(((bf16[8192,128]{1,0:T(8,128)(2,1)}), bf16[256,128]{1,0:T(8,128)(2,1)}) %reduce-scatter.5.cloned.1.call-update) | async-done | bytes 65552 | tf_op jit(solution)/shard_map/reduce_scatter | solution.py:92
  648.4 111.2 %all-reduce.5.cloned.1.call-done = f32[128,128]{1,0:T(8,128)} async-done(((f32[128,128]{1,0:T(8,128)}), f32[128,128]{1,0:T(8,128)}) %all-reduce.5.cloned.1.call-update) | async-done | bytes 65552 | tf_op jit(solution)/shard_map/psum | solution.py:86
  (134 shorter events, 99.0 us)
Async XLA Ops:
  7.2 217.9 %copy-start = (bf16[128,128]{1,0:T(8,128)(2,1)S(1)}, bf16[128,128]{1,0:T(8,128)(2,1)}, u32[]{:S(2)}) copy-start(bf16[128,128]{1,0:T(8,128)(2,1)} %param.15) | copy-start | bytes 98308
  7.2 88.8 %copy-start.3 = (s32[1,1,128]{2,1,0:T(1,128)S(1)}, s32[1,1,128]{2,1,0:T(1,128)}, u32[]{:S(2)}) copy-start(s32[1,1,128]{2,1,0:T(1,128)} %param.19) | copy-start | bytes 1540
  7.2 88.8 %copy-start.2 = (s32[1,1,128]{2,1,0:T(1,128)S(1)}, s32[1,1,128]{2,1,0:T(1,128)}, u32[]{:S(2)}) copy-start(s32[1,1,128]{2,1,0:T(1,128)} %param.18) | copy-start | bytes 1540
  7.2 88.5 %all-gather.3.cloned.1.call-start = ((), (), s32[]{:S(2)}) async-start(), calls=%async_computation.2 | async-start | bytes 2162688 | tf_op jit(solution)/shard_map/all_gather | solution.py:75
  9.5 215.5 %reduce-scatter.3.cloned.1.call-start = ((), (), s32[]{:S(2)}) async-start(), calls=%async_computation.3 | async-start | bytes 1114112 | tf_op jit(solution)/shard_map/reduce_scatter | solution.py:79
  162.7 62.3 %copy-start.4 = (bf16[256,128]{1,0:T(8,128)(2,1)S(1)}, bf16[256,128]{1,0:T(8,128)(2,1)}, u32[]{:S(2)}) copy-start(bf16[256,128]{1,0:T(8,128)(2,1)} %param.17) | copy-start | bytes 196612
  162.8 62.3 %copy-start.5 = (f32[128]{0:T(128)S(1)}, f32[128]{0:T(128)}, u32[]{:S(2)}) copy-start(f32[128]{0:T(128)} %param.16) | copy-start | bytes 1540
  163.9 106.8 %all-gather.5.cloned.1.call-start = ((), (), s32[]{:S(2)}) async-start(), calls=%async_computation.4 | async-start | bytes 1114112 | tf_op jit(solution)/shard_map/all_gather | solution.py:89
  227.7 212.0 %all-reduce.3.cloned.1.call-start = ((), (), s32[]{:S(2)}) async-start(), calls=%async_computation.6 | async-start | bytes 131072 | tf_op jit(solution)/shard_map/psum | solution.py:87
  229.5 417.3 %reduce-scatter.5.cloned.1.call-start = ((), (), s32[]{:S(2)}) async-start(), calls=%async_computation.5 | async-start | bytes 2162688 | tf_op jit(solution)/shard_map/reduce_scatter | solution.py:92
  270.7 2.5 copy-start.1
  341.1 418.5 %all-reduce.5.cloned.1.call-start = ((), (), s32[]{:S(2)}) async-start(), calls=%async_computation.7 | async-start | bytes 131072 | tf_op jit(solution)/shard_map/psum | solution.py:86
Sparse Core Ops, SparseCore 0:
  11.8 83.9 all-gather.2
  164.0 60.9 reduce-scatter.2
  227.8 42.9 all-gather.4
  274.6 146.0 all-reduce.2
  424.9 221.7 reduce-scatter.4
  649.0 110.5 all-reduce.4
